TPU v7x, 32 devices: a whole 2x2x4 slice. The times are simulated.
32 devices in a mesh: sample: 4 (over x, core), space: 8 (over z, y).
Axes of the slice: x: 2, y: 2, z: 4, core: 2. Of those that a mesh axis runs over, the one named last changes fastest.
Arguments:
- activations: bfloat16 [4, 64, 32, 1024], P('sample', 'space'), may hold values from -6 to 6
- open_cells: int32 [4, 64, 512], P('sample', 'space'), may hold values 0 or 1
- wind_class: int32 [4], P('sample'), may hold values from 0 to 7
- w_early: bfloat16 [3, 3, 3, 64, 128], replicated, may hold values from -0.15625 to 0.15625
- bias_table: float32 [8, 128], replicated, may hold values from -3 to 3
- w_deep: bfloat16 [2, 2, 2, 128, 256], replicated, may hold values from -0.1875 to 0.1875
- cotangent: bfloat16 [4, 16, 8, 1024], P('sample', 'space'), may hold values from -0.119628906 to 0.119628906
Outputs:
- deep: bfloat16 [4, 16, 8, 1024], P('sample', 'space')
- grad_deep: float32 [2, 2, 2, 128, 256], replicated
- grad_early: float32 [3, 3, 3, 64, 128], replicated
All inputs are finite; a program needn't handle non-finite values. No bound on the sum of `open_cells` on one device may be relied on, other than what follows from the above.
Results may differ from a plain program's by a relative error of at most 0.005.
Values may be sent and summed in bfloat16 or wider, within the bound.
No kernel may reach another device: no remote copies, remote signals or barrier semaphores. Data moves between devices by JAX's collectives and lax.ppermute only.
A program may use at most 64 MiB of HBM per device.

v0:
```python
import jax
import jax.numpy as jnp
from jax import lax
from jax.sharding import PartitionSpec as P

SLOPE = 0.3


def passed_along(value, axis, by):
    peers = lax.axis_size(axis)
    pairs = [(i, i + by) for i in range(peers) if 0 <= i + by < peers]
    return lax.ppermute(value, axis, pairs)


def early_forward(padded, w_early, bias):
    out = lax.conv_general_dilated(
        padded[None],
        w_early,
        (2, 2, 2),
        ((0, 0), (0, 0), (0, 0)),
        dimension_numbers=("NDHWC", "DHWIO", "NDHWC"),
        preferred_element_type=jnp.float32,
    )
    return out[0] + bias


def deep_terms(hidden, w_deep, upstream):
    zh, yh, xh, c1 = hidden.shape
    c2 = w_deep.shape[4]
    patches = (
        hidden.reshape(zh // 2, 2, yh // 2, 2, xh // 2, 2, c1)
        .transpose(0, 2, 4, 1, 3, 5, 6)
        .reshape(-1, 8 * c1)
    )
    out = jnp.dot(patches, w_deep.reshape(8 * c1, c2), preferred_element_type=jnp.float32)
    flat_up = upstream.reshape(-1, c2)
    grad_w = lax.dot_general(
        patches, flat_up, (((0,), (0,)), ((), ())), preferred_element_type=jnp.float32
    ).reshape(2, 2, 2, c1, c2)
    back = lax.dot_general(
        flat_up,
        w_deep.reshape(8, c1, c2),
        (((1,), (2,)), ((), ())),
        preferred_element_type=jnp.float32,
    )
    back = (
        back.reshape(zh // 2, yh // 2, xh // 2, 2, 2, 2, c1)
        .transpose(0, 3, 1, 4, 2, 5, 6)
        .reshape(zh, yh, xh, c1)
    )
    return (out, grad_w, back)


def early_grad(padded, delta):
    zo, yo, xo, c1 = delta.shape
    c0 = padded.shape[3]
    flat_delta = delta.reshape(-1, c1)
    pieces = []
    for a in range(3):
        for b in range(3):
            for c in range(3):
                piece = lax.slice(
                    padded,
                    (a, b, c, 0),
                    (a + 2 * zo - 1, b + 2 * yo - 1, c + 2 * xo - 1, c0),
                    (2, 2, 2, 1),
                ).reshape(-1, c0)
                pieces.append(
                    lax.dot_general(
                        piece,
                        flat_delta,
                        (((0,), (0,)), ((), ())),
                        preferred_element_type=jnp.float32,
                    )
                )
    return jnp.stack(pieces).reshape(3, 3, 3, c0, c1)


def total_terms(grad):
    flat = grad.reshape(-1)
    summed = lax.psum(flat, ("sample", "space"))
    return summed.reshape(grad.shape)


def body(activations, open_cells, wind_class, w_early, bias_table, w_deep, cotangent):
    depth = activations.shape[1]
    rows_y = activations.shape[2]
    chan_in = w_early.shape[3]
    chan_out = w_deep.shape[4]
    rows_x = activations.shape[3] // chan_in
    opens = open_cells[0].reshape(depth, rows_y, rows_x, 1).astype(jnp.bfloat16)
    masked = (activations[0].reshape(depth, rows_y, rows_x, chan_in) * opens).reshape(
        depth, rows_y, rows_x * chan_in
    )
    below = passed_along(masked[depth - 1], "space", 1)
    field = jnp.concatenate([below[None], masked], axis=0).reshape(
        depth + 1, rows_y, rows_x, chan_in
    )
    padded = jnp.pad(field, ((0, 0), (1, 0), (1, 0), (0, 0)))
    chosen = jnp.arange(bias_table.shape[0], dtype=jnp.int32)[:, None] == wind_class[0]
    bias = jnp.sum(jnp.where(chosen, bias_table, jnp.zeros_like(bias_table)), axis=0)
    pre = early_forward(padded, w_early, bias)
    hidden = jnp.where(pre > 0, pre, SLOPE * pre).astype(jnp.bfloat16)
    upstream = cotangent[0].reshape(depth // 4, rows_y // 4, rows_x // 4, chan_out)
    out, grad_w, back = deep_terms(hidden, w_deep, upstream)
    delta = (back * jnp.where(pre > 0, 1.0, SLOPE)).astype(jnp.bfloat16)
    grad_deep = total_terms(grad_w)
    grad_early = total_terms(early_grad(padded, delta))
    deep = out.astype(jnp.bfloat16).reshape(1, depth // 4, rows_y // 4, rows_x // 4 * chan_out)
    return (deep, grad_deep, grad_early)


def solution(mesh):
    in_specs = (
        P("sample", "space", None, None),
        P("sample", "space", None),
        P("sample"),
        P(),
        P(),
        P(),
        P("sample", "space", None, None),
    )
    out_specs = (P("sample", "space", None, None), P(), P())
    return jax.shard_map(body, mesh=mesh, in_specs=in_specs, out_specs=out_specs, check_vma=False)
```

profile of v0, /device:TPU:0, one launch (start us, length us, event | category | flops | bytes accessed | tf_op | source)
XLA Modules:
  0.0 380.3 jit_solution(18190275280594896844)
XLA Ops:
  7.2 1.8 reshape_squeeze.4
  10.9 4.9 %collective-permute-start = (bf16[32,1024]{1,0:T(8,128)(2,1)S(1)}, bf16[32,1024]{1,0:T(8,128)(2,1)S(1)}, u32[]{:S(2)}, u32[]{:S(2)}) collective-permute-start(bf16[32,1024]{1,0:T(8,128)(2,1)S(1)} %squeeze.11), channel_id=1, source_target_pairs={{0,1},{1,2},{2,3},{3,4},{4,5},{5,6},{6,7},{8,9},{9,10},{10,11},{11... | collective-permute-start | bytes 196616 | tf_op jit(solution)/shard_map/ppermute | solution.py:12
  17.9 1.8 fusion.111
  20.3 9.8 %slice.86 = bf16[4,16,8,64]{3,1,2,0:T(8,128)(2,1)} slice(bf16[9,33,17,64]{3,1,2,0:T(8,128)(2,1)S(1)} %fusion.11), slice={[0:7:2], [0:31:2], [0:15:2], [0:64:1]} | slice | bytes 131072 | tf_op jit(solution)/shard_map/slice | solution.py:62
  30.0 9.7 %slice.87 = bf16[4,16,8,64]{3,1,2,0:T(8,128)(2,1)} slice(bf16[9,33,17,64]{3,1,2,0:T(8,128)(2,1)S(1)} %fusion.11), slice={[0:7:2], [0:31:2], [1:16:2], [0:64:1]} | slice | bytes 131072 | tf_op jit(solution)/shard_map/slice | solution.py:62
  39.8 9.8 %slice.88 = bf16[4,16,8,64]{3,1,2,0:T(8,128)(2,1)} slice(bf16[9,33,17,64]{3,1,2,0:T(8,128)(2,1)S(1)} %fusion.11), slice={[0:7:2], [0:31:2], [2:17:2], [0:64:1]} | slice | bytes 131072 | tf_op jit(solution)/shard_map/slice | solution.py:62
  49.6 9.7 %slice.89 = bf16[4,16,8,64]{3,1,2,0:T(8,128)(2,1)} slice(bf16[9,33,17,64]{3,1,2,0:T(8,128)(2,1)S(1)} %fusion.11), slice={[0:7:2], [1:32:2], [0:15:2], [0:64:1]} | slice | bytes 131072 | tf_op jit(solution)/shard_map/slice | solution.py:62
  59.3 9.7 %slice.90 = bf16[4,16,8,64]{3,1,2,0:T(8,128)(2,1)} slice(bf16[9,33,17,64]{3,1,2,0:T(8,128)(2,1)S(1)} %fusion.11), slice={[0:7:2], [1:32:2], [1:16:2], [0:64:1]} | slice | bytes 131072 | tf_op jit(solution)/shard_map/slice | solution.py:62
  69.0 9.8 %slice.91 = bf16[4,16,8,64]{3,1,2,0:T(8,128)(2,1)} slice(bf16[9,33,17,64]{3,1,2,0:T(8,128)(2,1)S(1)} %fusion.11), slice={[0:7:2], [1:32:2], [2:17:2], [0:64:1]} | slice | bytes 131072 | tf_op jit(solution)/shard_map/slice | solution.py:62
  78.7 9.8 %slice.92 = bf16[4,16,8,64]{3,1,2,0:T(8,128)(2,1)} slice(bf16[9,33,17,64]{3,1,2,0:T(8,128)(2,1)S(1)} %fusion.11), slice={[0:7:2], [2:33:2], [0:15:2], [0:64:1]} | slice | bytes 131072 | tf_op jit(solution)/shard_map/slice | solution.py:62
  88.5 9.7 %slice.93 = bf16[4,16,8,64]{3,1,2,0:T(8,128)(2,1)} slice(bf16[9,33,17,64]{3,1,2,0:T(8,128)(2,1)S(1)} %fusion.11), slice={[0:7:2], [2:33:2], [1:16:2], [0:64:1]} | slice | bytes 131072 | tf_op jit(solution)/shard_map/slice | solution.py:62
  98.2 9.8 %slice.94 = bf16[4,16,8,64]{3,1,2,0:T(8,128)(2,1)} slice(bf16[9,33,17,64]{3,1,2,0:T(8,128)(2,1)S(1)} %fusion.11), slice={[0:7:2], [2:33:2], [2:17:2], [0:64:1]} | slice | bytes 131072 | tf_op jit(solution)/shard_map/slice | solution.py:62
  108.0 9.7 %slice.95 = bf16[4,16,8,64]{3,1,2,0:T(8,128)(2,1)} slice(bf16[9,33,17,64]{3,1,2,0:T(8,128)(2,1)S(1)} %fusion.11), slice={[1:8:2], [0:31:2], [0:15:2], [0:64:1]} | slice | bytes 131072 | tf_op jit(solution)/shard_map/slice | solution.py:62
  117.7 9.7 %slice.96 = bf16[4,16,8,64]{3,1,2,0:T(8,128)(2,1)} slice(bf16[9,33,17,64]{3,1,2,0:T(8,128)(2,1)S(1)} %fusion.11), slice={[1:8:2], [0:31:2], [1:16:2], [0:64:1]} | slice | bytes 131072 | tf_op jit(solution)/shard_map/slice | solution.py:62
  127.4 9.8 %slice.97 = bf16[4,16,8,64]{3,1,2,0:T(8,128)(2,1)} slice(bf16[9,33,17,64]{3,1,2,0:T(8,128)(2,1)S(1)} %fusion.11), slice={[1:8:2], [0:31:2], [2:17:2], [0:64:1]} | slice | bytes 131072 | tf_op jit(solution)/shard_map/slice | solution.py:62
  137.2 9.7 %slice.98 = bf16[4,16,8,64]{3,1,2,0:T(8,128)(2,1)} slice(bf16[9,33,17,64]{3,1,2,0:T(8,128)(2,1)S(1)} %fusion.11), slice={[1:8:2], [1:32:2], [0:15:2], [0:64:1]} | slice | bytes 131072 | tf_op jit(solution)/shard_map/slice | solution.py:62
  146.9 9.7 %slice.99 = bf16[4,16,8,64]{3,1,2,0:T(8,128)(2,1)} slice(bf16[9,33,17,64]{3,1,2,0:T(8,128)(2,1)S(1)} %fusion.11), slice={[1:8:2], [1:32:2], [1:16:2], [0:64:1]} | slice | bytes 131072 | tf_op jit(solution)/shard_map/slice | solution.py:62
  156.6 9.8 %slice.100 = bf16[4,16,8,64]{3,1,2,0:T(8,128)(2,1)} slice(bf16[9,33,17,64]{3,1,2,0:T(8,128)(2,1)S(1)} %fusion.11), slice={[1:8:2], [1:32:2], [2:17:2], [0:64:1]} | slice | bytes 131072 | tf_op jit(solution)/shard_map/slice | solution.py:62
  166.4 9.8 %slice.101 = bf16[4,16,8,64]{3,1,2,0:T(8,128)(2,1)} slice(bf16[9,33,17,64]{3,1,2,0:T(8,128)(2,1)S(1)} %fusion.11), slice={[1:8:2], [2:33:2], [0:15:2], [0:64:1]} | slice | bytes 131072 | tf_op jit(solution)/shard_map/slice | solution.py:62
  176.2 9.7 %slice.102 = bf16[4,16,8,64]{3,1,2,0:T(8,128)(2,1)} slice(bf16[9,33,17,64]{3,1,2,0:T(8,128)(2,1)S(1)} %fusion.11), slice={[1:8:2], [2:33:2], [1:16:2], [0:64:1]} | slice | bytes 131072 | tf_op jit(solution)/shard_map/slice | solution.py:62
  185.9 9.8 %slice.103 = bf16[4,16,8,64]{3,1,2,0:T(8,128)(2,1)} slice(bf16[9,33,17,64]{3,1,2,0:T(8,128)(2,1)S(1)} %fusion.11), slice={[1:8:2], [2:33:2], [2:17:2], [0:64:1]} | slice | bytes 131072 | tf_op jit(solution)/shard_map/slice | solution.py:62
  195.7 9.7 %slice.104 = bf16[4,16,8,64]{3,1,2,0:T(8,128)(2,1)} slice(bf16[9,33,17,64]{3,1,2,0:T(8,128)(2,1)S(1)} %fusion.11), slice={[2:9:2], [0:31:2], [0:15:2], [0:64:1]} | slice | bytes 131072 | tf_op jit(solution)/shard_map/slice | solution.py:62
  206.3 1.3 slice.106
  209.3 1.3 slice.109
  212.3 1.6 slice.112
  214.0 1.7 copy.51
  217.2 1.4 fusion.12
  219.8 1.2 fusion.41
  221.0 1.2 fusion.40
  233.4 1.3 fusion.50
  235.6 134.6 %all-reduce.4.cloned.1.call-done = (f32[2,2,2,128,256]{4,3,2,1,0:T(8,128)}, f32[3,3,3,64,128]{4,3,2,1,0:T(8,128)}) async-done(((f32[2,2,2,128,256]{4,3,2,1,0:T(8,128)}, f32[3,3,3,64,128]{4,3,2,1,0:T(8,128)}), (f32[2,2,2,128,256]{4,3,2,1,0:T(8,128)}, f32[3,3,3,64,128]{4,3,2,1,0:T(8,128)})) %all-reduce.4.cloned.1.call-update) | async-done | bytes 1933328 | tf_op jit(solution)/shard_map/psum | solution.py:81
  370.2 2.3 copy.90
  (103 shorter events, 23.5 us)
Async XLA Ops:
  7.2 9.4 %copy-start = (bf16[2,2,2,128,256]{4,3,2,1,0:T(8,128)(2,1)S(1)}, bf16[2,2,2,128,256]{4,3,2,1,0:T(8,128)(2,1)}, u32[]{:S(2)}) copy-start(bf16[2,2,2,128,256]{4,3,2,1,0:T(8,128)(2,1)} %param.12) | copy-start | bytes 1572868
  7.2 9.3 %copy-start.3 = (bf16[1,2,8,1024]{3,2,1,0:T(8,128)(2,1)S(1)}, bf16[1,2,8,1024]{3,2,1,0:T(8,128)(2,1)}, u32[]{:S(2)}) copy-start(bf16[1,2,8,1024]{3,2,1,0:T(8,128)(2,1)} %param.13) | copy-start | bytes 98308
  7.2 363.0 %all-reduce.4.cloned.1.call-start = ((), (), s32[]{:S(2)}) async-start(), calls=%async_computation | async-start | bytes 3866624 | tf_op jit(solution)/shard_map/psum | solution.py:81
  9.0 7.9 %copy-start.19 = (f32[8,128]{1,0:T(8,128)S(1)}, f32[8,128]{1,0:T(8,128)}, u32[]{:S(2)}) copy-start(f32[8,128]{1,0:T(8,128)} %param.11) | copy-start | bytes 12292
  10.9 6.8 %collective-permute-start = (bf16[32,1024]{1,0:T(8,128)(2,1)S(1)}, bf16[32,1024]{1,0:T(8,128)(2,1)S(1)}, u32[]{:S(2)}, u32[]{:S(2)}) collective-permute-start(bf16[32,1024]{1,0:T(8,128)(2,1)S(1)} %squeeze.11), channel_id=1, source_target_pairs={{0,1},{1,2},{2,3},{3,4},{4,5},{5,6},{6,7},{8,9},{9,10},{10,11},{11... | collective-permute-start | bytes 196616 | tf_op jit(solution)/shard_map/ppermute | solution.py:12
  216.2 1.0 copy-start.20
  216.2 1.0 copy-start.21
  218.6 3.7 copy-start.16
  218.6 4.9 %copy-start.15 = (bf16[4,16,8,64]{3,1,2,0:T(8,128)(2,1)S(1)}, bf16[4,16,8,64]{3,1,2,0:T(8,128)(2,1)}, u32[]{:S(2)}) copy-start(bf16[4,16,8,64]{3,1,2,0:T(8,128)(2,1)} %slice.89) | copy-start | bytes 196612
  218.6 6.0 %copy-start.14 = (bf16[4,16,8,64]{3,1,2,0:T(8,128)(2,1)S(1)}, bf16[4,16,8,64]{3,1,2,0:T(8,128)(2,1)}, u32[]{:S(2)}) copy-start(bf16[4,16,8,64]{3,1,2,0:T(8,128)(2,1)} %slice.90) | copy-start | bytes 196612
  218.6 6.2 %copy-start.13 = (bf16[4,16,8,64]{3,1,2,0:T(8,128)(2,1)S(1)}, bf16[4,16,8,64]{3,1,2,0:T(8,128)(2,1)}, u32[]{:S(2)}) copy-start(bf16[4,16,8,64]{3,1,2,0:T(8,128)(2,1)} %slice.91) | copy-start | bytes 196612
  219.5 5.1 %copy-start.17 = (bf16[4,16,8,128]{3,1,2,0:T(8,128)(2,1)S(1)}, bf16[4,16,8,128]{3,1,2,0:T(8,128)(2,1)}, u32[]{:S(2)}) copy-start(bf16[4,16,8,128]{3,1,2,0:T(8,128)(2,1)} %fusion.45) | copy-start | bytes 393220
  219.8 7.6 %copy-start.18 = (bf16[4,16,8,128]{3,1,2,0:T(8,128)(2,1)S(1)}, bf16[4,16,8,128]{3,1,2,0:T(8,128)(2,1)}, u32[]{:S(2)}) copy-start(bf16[4,16,8,128]{3,1,2,0:T(8,128)(2,1)} %fusion.45) | copy-start | bytes 393220
  219.8 9.8 %copy-start.12 = (bf16[4,16,8,64]{3,1,2,0:T(8,128)(2,1)S(1)}, bf16[4,16,8,64]{3,1,2,0:T(8,128)(2,1)}, u32[]{:S(2)}) copy-start(bf16[4,16,8,64]{3,1,2,0:T(8,128)(2,1)} %slice.96) | copy-start | bytes 196612
  221.0 8.8 %copy-start.11 = (bf16[4,16,8,64]{3,1,2,0:T(8,128)(2,1)S(1)}, bf16[4,16,8,64]{3,1,2,0:T(8,128)(2,1)}, u32[]{:S(2)}) copy-start(bf16[4,16,8,64]{3,1,2,0:T(8,128)(2,1)} %slice.97) | copy-start | bytes 196612
  222.3 7.8 %copy-start.10 = (bf16[4,16,8,64]{3,1,2,0:T(8,128)(2,1)S(1)}, bf16[4,16,8,64]{3,1,2,0:T(8,128)(2,1)}, u32[]{:S(2)}) copy-start(bf16[4,16,8,64]{3,1,2,0:T(8,128)(2,1)} %slice.98) | copy-start | bytes 196612
  223.4 6.9 %copy-start.9 = (bf16[4,16,8,64]{3,1,2,0:T(8,128)(2,1)S(1)}, bf16[4,16,8,64]{3,1,2,0:T(8,128)(2,1)}, u32[]{:S(2)}) copy-start(bf16[4,16,8,64]{3,1,2,0:T(8,128)(2,1)} %slice.99) | copy-start | bytes 196612
  224.6 5.9 %copy-start.8 = (bf16[4,16,8,64]{3,1,2,0:T(8,128)(2,1)S(1)}, bf16[4,16,8,64]{3,1,2,0:T(8,128)(2,1)}, u32[]{:S(2)}) copy-start(bf16[4,16,8,64]{3,1,2,0:T(8,128)(2,1)} %slice.100) | copy-start | bytes 196612
  224.8 5.9 %copy-start.7 = (bf16[4,16,8,64]{3,1,2,0:T(8,128)(2,1)S(1)}, bf16[4,16,8,64]{3,1,2,0:T(8,128)(2,1)}, u32[]{:S(2)}) copy-start(bf16[4,16,8,64]{3,1,2,0:T(8,128)(2,1)} %slice.101) | copy-start | bytes 196612
  225.0 5.9 %copy-start.6 = (bf16[4,16,8,64]{3,1,2,0:T(8,128)(2,1)S(1)}, bf16[4,16,8,64]{3,1,2,0:T(8,128)(2,1)}, u32[]{:S(2)}) copy-start(bf16[4,16,8,64]{3,1,2,0:T(8,128)(2,1)} %slice.102) | copy-start | bytes 196612
  226.2 5.0 %copy-start.5 = (bf16[4,16,8,64]{3,1,2,0:T(8,128)(2,1)S(1)}, bf16[4,16,8,64]{3,1,2,0:T(8,128)(2,1)}, u32[]{:S(2)}) copy-start(bf16[4,16,8,64]{3,1,2,0:T(8,128)(2,1)} %slice.103) | copy-start | bytes 196612
  227.4 4.0 %copy-start.4 = (bf16[4,16,8,64]{3,1,2,0:T(8,128)(2,1)S(1)}, bf16[4,16,8,64]{3,1,2,0:T(8,128)(2,1)}, u32[]{:S(2)}) copy-start(bf16[4,16,8,64]{3,1,2,0:T(8,128)(2,1)} %slice.104) | copy-start | bytes 196612
  233.4 1.3 copy-start.2
  370.2 2.4 copy-start.1
Sparse Core Ops, SparseCore 0:
  234.8 135.3 all-reduce.3
where the time goes:
time: 381 us; the launch traced here: 380 us
  local copies, waits for them, and re-layouts  204 us (54%)
  waiting for transfers between devices  135 us (35%)
  matrix products  16.5 us (4%)
  between operations  15.2 us (4%)
  starting transfers between devices  4.91 us (1%)
  other arithmetic  4.8 us (1%)
    slice x27, local copies, waits for them, and re-layouts, early_grad(): lax.slice(padded, (a, b, c, 0), (a + 2 * zo - 1, b + 2 * yo - 1, c + 2 *...  194 us
    psum x1, waiting for transfers between devices, total_terms(): summed = lax.psum(flat, ('sample', 'space'))  135 us
    dot_general x27, matrix products, early_grad(): lax.dot_general(piece, flat_delta, (((0,), (0,)), ((), ())), preferred_el...  13.3 us
  transfers between devices with their start and end apart: 2, of which 2 were waited for; matrix products, arithmetic and copies ran while one was open for 0% of the time, Pallas kernels for 0%

commit v1 on v0

--- a/solution.py
+++ b/solution.py
@@ -78,7 +78,7 @@
 
 def total_terms(grad):
     flat = grad.reshape(-1)
-    summed = lax.psum(flat, ("sample", "space"))
+    summed = lax.psum(lax.psum(flat, "space"), "sample")
     return summed.reshape(grad.shape)
 
 

time: 381 us -> 393 us (1.031)
  waiting for transfers between devices: 135 us -> 150 us
  matrix products: 16.5 us -> 9.76 us
  local copies, waits for them, and re-layouts: 204 us -> 208 us
    psum x1 -> x2, waiting for transfers between devices: 135 us -> 149 us  [total_terms(): summed = lax.psum(lax.psum(flat, 'space'), 'sample')]
    dot_general x27, matrix products: 13.3 us -> 7.57 us  [early_grad(): lax.dot_general(piece, flat_delta, (((0,), (0,)), ((), ())), preferred_el...]
  transfers between devices with their start and end apart: 2 -> 3, of which waited for: 2 -> 3; matrix products, arithmetic and copies ran while one was open for 0% -> 0% of each run, Pallas kernels for 0% -> 0%
where the time goes in v1:
time: 393 us
  local copies, waits for them, and re-layouts  208 us (53%)
  waiting for transfers between devices  150 us (38%)
  between operations  15.2 us (4%)
  matrix products  9.76 us (2%)
  starting transfers between devices  4.95 us (1%)
  other arithmetic  4.8 us (1%)
    slice x27, local copies, waits for them, and re-layouts, early_grad(): lax.slice(padded, (a, b, c, 0), (a + 2 * zo - 1, b + 2 * yo - 1, c + 2 *...  194 us
    psum x2, waiting for transfers between devices, total_terms(): summed = lax.psum(lax.psum(flat, 'space'), 'sample')  149 us
  transfers between devices with their start and end apart: 3, of which 3 were waited for; matrix products, arithmetic and copies ran while one was open for 0% of the time, Pallas kernels for 0%

profile of v1, /device:TPU:0, one launch (start us, length us, event | category | flops | bytes accessed | tf_op | source)
XLA Modules:
  0.0 393.0 jit_solution(12593855095702489543)
XLA Ops:
  7.2 1.8 reshape_squeeze.4
  10.9 4.9 %collective-permute-start = (bf16[32,1024]{1,0:T(8,128)(2,1)S(1)}, bf16[32,1024]{1,0:T(8,128)(2,1)S(1)}, u32[]{:S(2)}, u32[]{:S(2)}) collective-permute-start(bf16[32,1024]{1,0:T(8,128)(2,1)S(1)} %squeeze.11), channel_id=1, source_target_pairs={{0,1},{1,2},{2,3},{3,4},{4,5},{5,6},{6,7},{8,9},{9,10},{10,11},{11... | collective-permute-start | bytes 196616 | tf_op jit(solution)/shard_map/ppermute | solution.py:12
  17.9 1.8 fusion.110
  20.2 9.8 %slice.86 = bf16[4,16,8,64]{3,1,2,0:T(8,128)(2,1)} slice(bf16[9,33,17,64]{3,1,2,0:T(8,128)(2,1)S(1)} %fusion.11), slice={[0:7:2], [0:31:2], [0:15:2], [0:64:1]} | slice | bytes 131072 | tf_op jit(solution)/shard_map/slice | solution.py:62
  30.0 9.7 %slice.87 = bf16[4,16,8,64]{3,1,2,0:T(8,128)(2,1)} slice(bf16[9,33,17,64]{3,1,2,0:T(8,128)(2,1)S(1)} %fusion.11), slice={[0:7:2], [0:31:2], [1:16:2], [0:64:1]} | slice | bytes 131072 | tf_op jit(solution)/shard_map/slice | solution.py:62
  39.8 9.7 %slice.88 = bf16[4,16,8,64]{3,1,2,0:T(8,128)(2,1)} slice(bf16[9,33,17,64]{3,1,2,0:T(8,128)(2,1)S(1)} %fusion.11), slice={[0:7:2], [0:31:2], [2:17:2], [0:64:1]} | slice | bytes 131072 | tf_op jit(solution)/shard_map/slice | solution.py:62
  49.5 9.7 %slice.89 = bf16[4,16,8,64]{3,1,2,0:T(8,128)(2,1)} slice(bf16[9,33,17,64]{3,1,2,0:T(8,128)(2,1)S(1)} %fusion.11), slice={[0:7:2], [1:32:2], [0:15:2], [0:64:1]} | slice | bytes 131072 | tf_op jit(solution)/shard_map/slice | solution.py:62
  59.2 9.7 %slice.90 = bf16[4,16,8,64]{3,1,2,0:T(8,128)(2,1)} slice(bf16[9,33,17,64]{3,1,2,0:T(8,128)(2,1)S(1)} %fusion.11), slice={[0:7:2], [1:32:2], [1:16:2], [0:64:1]} | slice | bytes 131072 | tf_op jit(solution)/shard_map/slice | solution.py:62
  68.9 9.8 %slice.91 = bf16[4,16,8,64]{3,1,2,0:T(8,128)(2,1)} slice(bf16[9,33,17,64]{3,1,2,0:T(8,128)(2,1)S(1)} %fusion.11), slice={[0:7:2], [1:32:2], [2:17:2], [0:64:1]} | slice | bytes 131072 | tf_op jit(solution)/shard_map/slice | solution.py:62
  78.7 9.8 %slice.92 = bf16[4,16,8,64]{3,1,2,0:T(8,128)(2,1)} slice(bf16[9,33,17,64]{3,1,2,0:T(8,128)(2,1)S(1)} %fusion.11), slice={[0:7:2], [2:33:2], [0:15:2], [0:64:1]} | slice | bytes 131072 | tf_op jit(solution)/shard_map/slice | solution.py:62
  88.5 9.8 %slice.93 = bf16[4,16,8,64]{3,1,2,0:T(8,128)(2,1)} slice(bf16[9,33,17,64]{3,1,2,0:T(8,128)(2,1)S(1)} %fusion.11), slice={[0:7:2], [2:33:2], [1:16:2], [0:64:1]} | slice | bytes 131072 | tf_op jit(solution)/shard_map/slice | solution.py:62
  98.2 9.8 %slice.94 = bf16[4,16,8,64]{3,1,2,0:T(8,128)(2,1)} slice(bf16[9,33,17,64]{3,1,2,0:T(8,128)(2,1)S(1)} %fusion.11), slice={[0:7:2], [2:33:2], [2:17:2], [0:64:1]} | slice | bytes 131072 | tf_op jit(solution)/shard_map/slice | solution.py:62
  108.0 9.7 %slice.95 = bf16[4,16,8,64]{3,1,2,0:T(8,128)(2,1)} slice(bf16[9,33,17,64]{3,1,2,0:T(8,128)(2,1)S(1)} %fusion.11), slice={[1:8:2], [0:31:2], [0:15:2], [0:64:1]} | slice | bytes 131072 | tf_op jit(solution)/shard_map/slice | solution.py:62
  117.8 9.7 %slice.96 = bf16[4,16,8,64]{3,1,2,0:T(8,128)(2,1)} slice(bf16[9,33,17,64]{3,1,2,0:T(8,128)(2,1)S(1)} %fusion.11), slice={[1:8:2], [0:31:2], [1:16:2], [0:64:1]} | slice | bytes 131072 | tf_op jit(solution)/shard_map/slice | solution.py:62
  127.5 9.8 %slice.97 = bf16[4,16,8,64]{3,1,2,0:T(8,128)(2,1)} slice(bf16[9,33,17,64]{3,1,2,0:T(8,128)(2,1)S(1)} %fusion.11), slice={[1:8:2], [0:31:2], [2:17:2], [0:64:1]} | slice | bytes 131072 | tf_op jit(solution)/shard_map/slice | solution.py:62
  137.2 9.7 %slice.98 = bf16[4,16,8,64]{3,1,2,0:T(8,128)(2,1)} slice(bf16[9,33,17,64]{3,1,2,0:T(8,128)(2,1)S(1)} %fusion.11), slice={[1:8:2], [1:32:2], [0:15:2], [0:64:1]} | slice | bytes 131072 | tf_op jit(solution)/shard_map/slice | solution.py:62
  147.0 9.7 %slice.99 = bf16[4,16,8,64]{3,1,2,0:T(8,128)(2,1)} slice(bf16[9,33,17,64]{3,1,2,0:T(8,128)(2,1)S(1)} %fusion.11), slice={[1:8:2], [1:32:2], [1:16:2], [0:64:1]} | slice | bytes 131072 | tf_op jit(solution)/shard_map/slice | solution.py:62
  156.7 9.8 %slice.100 = bf16[4,16,8,64]{3,1,2,0:T(8,128)(2,1)} slice(bf16[9,33,17,64]{3,1,2,0:T(8,128)(2,1)S(1)} %fusion.11), slice={[1:8:2], [1:32:2], [2:17:2], [0:64:1]} | slice | bytes 131072 | tf_op jit(solution)/shard_map/slice | solution.py:62
  166.4 9.7 %slice.101 = bf16[4,16,8,64]{3,1,2,0:T(8,128)(2,1)} slice(bf16[9,33,17,64]{3,1,2,0:T(8,128)(2,1)S(1)} %fusion.11), slice={[1:8:2], [2:33:2], [0:15:2], [0:64:1]} | slice | bytes 131072 | tf_op jit(solution)/shard_map/slice | solution.py:62
  176.2 9.7 %slice.102 = bf16[4,16,8,64]{3,1,2,0:T(8,128)(2,1)} slice(bf16[9,33,17,64]{3,1,2,0:T(8,128)(2,1)S(1)} %fusion.11), slice={[1:8:2], [2:33:2], [1:16:2], [0:64:1]} | slice | bytes 131072 | tf_op jit(solution)/shard_map/slice | solution.py:62
  185.9 9.8 %slice.103 = bf16[4,16,8,64]{3,1,2,0:T(8,128)(2,1)} slice(bf16[9,33,17,64]{3,1,2,0:T(8,128)(2,1)S(1)} %fusion.11), slice={[1:8:2], [2:33:2], [2:17:2], [0:64:1]} | slice | bytes 131072 | tf_op jit(solution)/shard_map/slice | solution.py:62
  195.7 9.7 %slice.104 = bf16[4,16,8,64]{3,1,2,0:T(8,128)(2,1)} slice(bf16[9,33,17,64]{3,1,2,0:T(8,128)(2,1)S(1)} %fusion.11), slice={[2:9:2], [0:31:2], [0:15:2], [0:64:1]} | slice | bytes 131072 | tf_op jit(solution)/shard_map/slice | solution.py:62
  206.2 1.3 slice.106
  209.2 1.3 slice.109
  212.3 1.6 slice.112
  213.9 1.7 copy.51
  217.1 1.4 fusion.12
  220.1 1.5 copy.52
  230.4 100.6 %all-reduce.6.cloned.1.call-done = (f32[262144]{0:T(1024)}, f32[221184]{0:T(1024)}) async-done(((f32[262144]{0:T(1024)}, f32[221184]{0:T(1024)}), (f32[262144]{0:T(1024)}, f32[221184]{0:T(1024)})) %all-reduce.6.cloned.1.call-update) | async-done | bytes 1933328 | tf_op jit(solution)/shard_map/psum | solution.py:81
  331.0 2.5 reshape.87
  334.4 48.5 %all-reduce.8.cloned.1.call-done = (f32[2,2,2,128,256]{4,3,2,1,0:T(8,128)}, f32[3,3,3,64,128]{4,3,2,1,0:T(8,128)}) async-done(((f32[2,2,2,128,256]{4,3,2,1,0:T(8,128)}, f32[3,3,3,64,128]{4,3,2,1,0:T(8,128)}), (f32[2,2,2,128,256]{4,3,2,1,0:T(8,128)}, f32[3,3,3,64,128]{4,3,2,1,0:T(8,128)})) %all-reduce.8.cloned.1.call-update) | async-done | bytes 1933328 | tf_op jit(solution)/shard_map/psum | solution.py:81
  382.9 2.3 copy.93
  (114 shorter events, 21.5 us)
Async XLA Ops:
  7.2 9.4 %copy-start = (bf16[2,2,2,128,256]{4,3,2,1,0:T(8,128)(2,1)S(1)}, bf16[2,2,2,128,256]{4,3,2,1,0:T(8,128)(2,1)}, u32[]{:S(2)}) copy-start(bf16[2,2,2,128,256]{4,3,2,1,0:T(8,128)(2,1)} %param.12) | copy-start | bytes 1572868
  7.2 9.3 %copy-start.3 = (bf16[1,2,8,1024]{3,2,1,0:T(8,128)(2,1)S(1)}, bf16[1,2,8,1024]{3,2,1,0:T(8,128)(2,1)}, u32[]{:S(2)}) copy-start(bf16[1,2,8,1024]{3,2,1,0:T(8,128)(2,1)} %param.13) | copy-start | bytes 98308
  7.2 323.8 %all-reduce.6.cloned.1.call-start = ((), (), s32[]{:S(2)}) async-start(), calls=%async_computation | async-start | bytes 3866624 | tf_op jit(solution)/shard_map/psum | solution.py:81
  9.0 7.9 %copy-start.22 = (f32[8,128]{1,0:T(8,128)S(1)}, f32[8,128]{1,0:T(8,128)}, u32[]{:S(2)}) copy-start(f32[8,128]{1,0:T(8,128)} %param.11) | copy-start | bytes 12292
  10.9 6.8 %collective-permute-start = (bf16[32,1024]{1,0:T(8,128)(2,1)S(1)}, bf16[32,1024]{1,0:T(8,128)(2,1)S(1)}, u32[]{:S(2)}, u32[]{:S(2)}) collective-permute-start(bf16[32,1024]{1,0:T(8,128)(2,1)S(1)} %squeeze.11), channel_id=1, source_target_pairs={{0,1},{1,2},{2,3},{3,4},{4,5},{5,6},{6,7},{8,9},{9,10},{10,11},{11... | collective-permute-start | bytes 196616 | tf_op jit(solution)/shard_map/ppermute | solution.py:12
  216.1 1.0 copy-start.23
  216.1 1.0 copy-start.24
  219.4 4.5 %copy-start.20 = (bf16[4,16,8,64]{3,1,2,0:T(8,128)(2,1)S(1)}, bf16[4,16,8,64]{3,1,2,0:T(8,128)(2,1)}, u32[]{:S(2)}) copy-start(bf16[4,16,8,64]{3,1,2,0:T(8,128)(2,1)} %slice.88) | copy-start | bytes 196612
  219.7 1.9 copy-start.21
  219.7 4.4 %copy-start.19 = (bf16[4,16,8,64]{3,1,2,0:T(8,128)(2,1)S(1)}, bf16[4,16,8,64]{3,1,2,0:T(8,128)(2,1)}, u32[]{:S(2)}) copy-start(bf16[4,16,8,64]{3,1,2,0:T(8,128)(2,1)} %slice.89) | copy-start | bytes 196612
  219.7 4.7 %copy-start.18 = (bf16[4,16,8,64]{3,1,2,0:T(8,128)(2,1)S(1)}, bf16[4,16,8,64]{3,1,2,0:T(8,128)(2,1)}, u32[]{:S(2)}) copy-start(bf16[4,16,8,64]{3,1,2,0:T(8,128)(2,1)} %slice.90) | copy-start | bytes 196612
  220.1 4.6 %copy-start.17 = (bf16[4,16,8,64]{3,1,2,0:T(8,128)(2,1)S(1)}, bf16[4,16,8,64]{3,1,2,0:T(8,128)(2,1)}, u32[]{:S(2)}) copy-start(bf16[4,16,8,64]{3,1,2,0:T(8,128)(2,1)} %slice.91) | copy-start | bytes 196612
  220.1 4.8 %copy-start.16 = (bf16[4,16,8,64]{3,1,2,0:T(8,128)(2,1)S(1)}, bf16[4,16,8,64]{3,1,2,0:T(8,128)(2,1)}, u32[]{:S(2)}) copy-start(bf16[4,16,8,64]{3,1,2,0:T(8,128)(2,1)} %slice.92) | copy-start | bytes 196612
  220.1 5.0 %copy-start.15 = (bf16[4,16,8,64]{3,1,2,0:T(8,128)(2,1)S(1)}, bf16[4,16,8,64]{3,1,2,0:T(8,128)(2,1)}, u32[]{:S(2)}) copy-start(bf16[4,16,8,64]{3,1,2,0:T(8,128)(2,1)} %slice.93) | copy-start | bytes 196612
  221.6 3.7 copy-start.14
  221.6 3.9 copy-start.13
  221.6 4.1 %copy-start.12 = (bf16[4,16,8,64]{3,1,2,0:T(8,128)(2,1)S(1)}, bf16[4,16,8,64]{3,1,2,0:T(8,128)(2,1)}, u32[]{:S(2)}) copy-start(bf16[4,16,8,64]{3,1,2,0:T(8,128)(2,1)} %slice.96) | copy-start | bytes 196612
  222.8 3.2 copy-start.11
  224.0 2.3 copy-start.10
  224.2 2.2 copy-start.9
  224.4 2.2 copy-start.8
  224.6 2.2 copy-start.7
  224.9 2.2 copy-start.6
  225.1 2.2 copy-start.5
  225.3 2.2 copy-start.4
  229.4 0.9 copy-start.2
  230.4 152.5 %all-reduce.8.cloned.1.call-start = ((), (), s32[]{:S(2)}) async-start(), calls=%async_computation.1 | async-start | bytes 3866624 | tf_op jit(solution)/shard_map/psum | solution.py:81
  382.9 2.4 copy-start.1
Sparse Core Ops, SparseCore 0:
  230.5 100.4 all-reduce.5
  334.2 48.5 all-reduce.7
